TPU v7x, 32 devices: a whole 2x2x4 slice. The times are simulated.
32 devices in a mesh: expert: 8 (over y, x, core), tensor: 4 (over z).
Axes of the slice: x: 2, y: 2, z: 4, core: 2. Of those that a mesh axis runs over, the one named last changes fastest.
Arguments:
- tokens: bfloat16 [512, 4096], P(('expert', 'tensor')), may hold values from -6 to 6
- grad_out: bfloat16 [512, 4096], P(('expert', 'tensor')), may hold values from -1.5 to 1.5
- routes: int32 [512, 8], P(('expert', 'tensor')), may hold values from 0 to 15, all different within a row; in each aligned block of 16 rows (0 to 15, 16 to 31, ...) at most 12 rows name the same one
- gate_probs: bfloat16 [512, 8], P(('expert', 'tensor')), may hold values from 0.019897461 to 0.29882812
- w_gate: bfloat16 [16, 1536, 4096], P('expert', 'tensor'), may hold values from -0.09375 to 0.09375
- w_up: bfloat16 [16, 1536, 4096], P('expert', 'tensor'), may hold values from -0.09375 to 0.09375
- w_down: bfloat16 [16, 1536, 4096], P('expert', 'tensor'), may hold values from -0.15625 to 0.15625
Outputs:
- d_tokens: bfloat16 [512, 4096], P(('expert', 'tensor'))
- d_probs: bfloat16 [512, 8], P(('expert', 'tensor'))
- d_gate: bfloat16 [16, 1536, 4096], P('expert', 'tensor')
- d_up: bfloat16 [16, 1536, 4096], P('expert', 'tensor')
- d_down: bfloat16 [16, 1536, 4096], P('expert', 'tensor')
Inputs may be any that keep to these rules, and one draw needn't show every extreme that they name: `routes`: each token names 8 different experts. In each aligned block of 16 tokens (the tokens of one device) no expert is named by more than 12 tokens, a bound that some block reaches.
All inputs are finite; a program needn't handle non-finite values.
Results may differ from a plain program's by a relative error of at most 0.019.
Values may be sent and summed in bfloat16 or wider, within the bound.
A program may use at most 256 MiB of HBM per device.

v0:
```python
import jax
import jax.numpy as jnp
from jax import lax
from jax.sharding import PartitionSpec as P

AXES = ("expert", "tensor")


def per_device(tokens, grad_out, routes, gate_probs, w_gate, w_up, w_down):
    local, units, width = w_gate.shape
    first = lax.axis_index("expert") * local
    mine = first + jnp.arange(local, dtype=jnp.int32)
    owners = lax.axis_size("expert")
    ids = jnp.arange(local * owners, dtype=jnp.int32)
    hit = routes[:, :, None] == ids[None, None, :]
    table = jnp.sum(jnp.where(hit, gate_probs[:, :, None].astype(jnp.float32), 0.0), axis=1)
    table = table.astype(jnp.bfloat16)
    rows_x = lax.all_gather(tokens, AXES, axis=0, tiled=True)
    rows_g = lax.all_gather(grad_out, AXES, axis=0, tiled=True)
    probs = lax.all_gather(table, AXES, axis=0, tiled=True)
    probs = lax.dynamic_slice_in_dim(probs, first, local, axis=1).astype(jnp.float32)
    count = rows_x.shape[0]
    wg = w_gate.reshape(local * units, width)
    wu = w_up.reshape(local * units, width)
    wd = w_down.reshape(local * units, width)
    nt = (((1,), (1,)), ((), ()))
    tn = (((0,), (0,)), ((), ()))
    f32 = jnp.float32
    gate = lax.dot_general(rows_x, wg, nt, preferred_element_type=f32)
    up = lax.dot_general(rows_x, wu, nt, preferred_element_type=f32)
    back = lax.dot_general(rows_g, wd, nt, preferred_element_type=f32)
    sigma = jax.nn.sigmoid(gate)
    act = gate * sigma
    hidden = act * up
    p = jnp.broadcast_to(probs[:, :, None], (count, local, units)).reshape(count, local * units)
    d_hidden = p * back
    dgp = (d_hidden * up * sigma * (1.0 + gate * (1.0 - sigma))).astype(jnp.bfloat16)
    dup = (d_hidden * act).astype(jnp.bfloat16)
    hs = (hidden * p).astype(jnp.bfloat16)
    dprob = jnp.sum((hidden * back).reshape(count, local, units), axis=2)
    part = lax.dot_general(dgp, wg, (((1,), (0,)), ((), ())), preferred_element_type=f32)
    part = part + lax.dot_general(dup, wu, (((1,), (0,)), ((), ())), preferred_element_type=f32)
    d_tokens = lax.psum_scatter(part.astype(jnp.bfloat16), AXES, scatter_dimension=0, tiled=True)
    d_gate = lax.dot_general(dgp, rows_x, tn, preferred_element_type=f32).astype(jnp.bfloat16)
    d_up = lax.dot_general(dup, rows_x, tn, preferred_element_type=f32).astype(jnp.bfloat16)
    d_down = lax.dot_general(hs, rows_g, tn, preferred_element_type=f32).astype(jnp.bfloat16)
    wide = lax.dynamic_update_slice(jnp.zeros((count, local * owners), f32), dprob, (0, first))
    mineprob = lax.psum_scatter(wide.astype(jnp.bfloat16), AXES, scatter_dimension=0, tiled=True)
    d_probs = jnp.sum(jnp.where(hit, mineprob.astype(f32)[:, None, :], 0.0), axis=2).astype(
        jnp.bfloat16
    )
    shape = (local, units, width)
    return (d_tokens, d_probs, d_gate.reshape(shape), d_up.reshape(shape), d_down.reshape(shape))


def solution(mesh):
    tok = P(AXES, None)
    wt = P("expert", "tensor", None)
    return jax.shard_map(
        per_device,
        mesh=mesh,
        in_specs=(tok, tok, tok, tok, wt, wt, wt),
        out_specs=(tok, tok, wt, wt, wt),
        check_vma=False,
    )
```

profile of v0, /device:TPU:0, one launch (start us, length us, event | category | flops | bytes accessed | tf_op | source)
XLA Modules:
  0.0 514.9 jit_solution(6247129796937112394)
XLA Ops:
  7.2 0.7 all-gather.5.cloned.1.call-update
  7.9 0.7 all-gather.3.cloned.1.call-update
  8.7 67.1 %all-gather.5.cloned.1.call-done = bf16[512,4096]{1,0:T(8,128)(2,1)} async-done(((bf16[16,4096]{1,0:T(8,128)(2,1)}), bf16[512,4096]{1,0:T(8,128)(2,1)}) %all-gather.5.cloned.1.call-update) | async-done | bytes 4194320 | tf_op jit(solution)/shard_map/all_gather | solution.py:18
  75.8 8.8 %fusion.3 = f32[512,768]{1,0:T(8,128)} fusion(bf16[512,4096]{1,0:T(8,128)(2,1)} %all-gather.5.cloned.1.call-done, bf16[768,4096]{1,0:T(8,128)(2,1)} %bitcast.33), kind=kOutput, calls=%fused_computation.15 | convolution fusion | flops 3221225472 | bytes 12058624 | tf_op jit(solution)/shard_map/dot_general | solution.py:30
  84.6 4.8 fusion.4
  89.5 50.0 %all-gather.3.cloned.1.call-done = bf16[512,4096]{1,0:T(8,128)(2,1)} async-done(((bf16[16,4096]{1,0:T(8,128)(2,1)}), bf16[512,4096]{1,0:T(8,128)(2,1)}) %all-gather.3.cloned.1.call-update) | async-done | bytes 4194320 | tf_op jit(solution)/shard_map/all_gather | solution.py:19
  139.5 9.5 %multiply_multiply_fusion = (f32[512,768]{1,0:T(8,128)S(1)}, f32[512,768]{1,0:T(8,128)}) fusion(f32[512,768]{1,0:T(8,128)} %fusion.3, f32[512,768]{1,0:T(8,128)} %fusion.4, bf16[512,4096]{1,0:T(8,128)(2,1)} %all-gather.3.cloned.1.call-done, bf16[768,4096]{1,0:T(8,128)(2,1)} %bitcast.32), kind=kOutput, calls=%fused_computation.10 | convolution fusion | flops 3223584768 | bytes 16777216 | tf_op jit(solution)/shard_map/dot_general | solution.py:31
  149.0 0.8 reshape.43
  149.8 0.7 reduce_sum.28
  151.0 0.6 copy-done.5
  151.9 132.3 %reduce-scatter.5.cloned.1.call-done = bf16[16,16]{1,0:T(8,128)(2,1)} async-done(((bf16[512,16]{1,0:T(8,128)(2,1)}), bf16[16,16]{1,0:T(8,128)(2,1)}) %reduce-scatter.5.cloned.1.call-update) | async-done | bytes 528 | tf_op jit(solution)/shard_map/reduce_scatter | solution.py:48
  284.2 0.8 convert_element_type.47
  285.2 64.8 %all_gather.9 = bf16[512,16]{1,0:T(8,128)(2,1)S(1)} all-gather(bf16[16,16]{1,0:T(8,128)(2,1)S(1)} %get-tuple-element.11), channel_id=1, replica_groups=mesh['expert'=8,'tensor'=4] {'expert','tensor'}, dimensions={0}, use_global_device_ids=true | all-gather | bytes 16896 | tf_op jit(solution)/shard_map/all_gather | solution.py:20
  350.1 0.6 broadcast_in_dim.37
  350.9 0.9 multiply_convert_fusion.1
  351.8 0.5 slice-done.2
  352.3 0.9 slice-done.3
  353.2 3.5 fusion.5
  356.7 5.1 add_convert_fusion
  361.7 0.7 copy.16
  362.4 7.7 %convolution_convert_fusion.2 = bf16[768,4096]{1,0:T(8,128)(2,1)} fusion(bf16[512,768]{1,0:T(8,128)(2,1)S(1)} %get-tuple-element.13, bf16[512,4096]{1,0:T(8,128)(2,1)} %all-gather.5.cloned.1.call-done), kind=kOutput, calls=%fused_computation.3 | convolution fusion | flops 3224371200 | bytes 11272192 | tf_op jit(solution)/shard_map/dot_general | solution.py:44
  370.1 5.4 %convolution_convert_fusion.1 = bf16[768,4096]{1,0:T(8,128)(2,1)} fusion(bf16[512,768]{1,0:T(8,128)(2,1)S(1)} %get-tuple-element.12, bf16[512,4096]{1,0:T(8,128)(2,1)S(1)} %copy-done.9), kind=kOutput, calls=%fused_computation.2 | convolution fusion | flops 3224371200 | bytes 11272192 | tf_op jit(solution)/shard_map/dot_general | solution.py:45
  375.5 5.6 %convolution_convert_fusion = bf16[768,4096]{1,0:T(8,128)(2,1)} fusion(bf16[512,4096]{1,0:T(8,128)(2,1)S(1)} %copy-done.10, f32[512,768]{1,0:T(8,128)S(1)} %bitcast.31, f32[512,768]{1,0:T(8,128)S(1)} %copy-done.1, f32[512,768]{1,0:T(8,128)S(1)} %copy-done.3), kind=kOutput, calls=%fused_computation.1 | convolution fusion | flops 3227123712 | bytes 15204352 | tf_op jit(solution)/shard_map/dot_general | solution.py:46
  381.1 127.3 %reduce-scatter.3.cloned.1.call-done = bf16[16,4096]{1,0:T(8,128)(2,1)} async-done(((bf16[512,4096]{1,0:T(8,128)(2,1)}), bf16[16,4096]{1,0:T(8,128)(2,1)}) %reduce-scatter.3.cloned.1.call-update) | async-done | bytes 131088 | tf_op jit(solution)/shard_map/reduce_scatter | solution.py:43
  (47 shorter events, 1.2 us)
Async XLA Ops:
  7.2 68.7 %all-gather.5.cloned.1.call-start = ((), (), s32[]{:S(2)}) async-start(), calls=%async_computation.3 | async-start | bytes 4325376 | tf_op jit(solution)/shard_map/all_gather | solution.py:18
  7.2 77.4 %slice-start = ((s8[6291456]{0:T(1024)(128)(4,1)}), s8[2097152]{0:T(1024)(128)(4,1)S(1)}, s32[]{:S(2)}) async-start(s8[6291456]{0:T(1024)(128)(4,1)} %bitcast.24), calls=%async_computation.6 | async-start | bytes 4194304
  7.9 131.6 %all-gather.3.cloned.1.call-start = ((), (), s32[]{:S(2)}) async-start(), calls=%async_computation.2 | async-start | bytes 4325376 | tf_op jit(solution)/shard_map/all_gather | solution.py:19
  8.6 275.5 %reduce-scatter.5.cloned.1.call-start = ((), (), s32[]{:S(2)}) async-start(), calls=%async_computation.5 | async-start | bytes 135168 | tf_op jit(solution)/shard_map/reduce_scatter | solution.py:48
  75.8 8.8 %slice-start.1 = ((s8[6291456]{0:T(1024)(128)(4,1)}), s8[4194304]{0:T(1024)(128)(4,1)S(1)}, s32[]{:S(2)}) async-start(s8[6291456]{0:T(1024)(128)(4,1)} %bitcast.24), calls=%async_computation.7 | async-start | bytes 8388608
  75.8 8.8 %copy-start.8 = (bf16[512,4096]{1,0:T(8,128)(2,1)S(1)}, bf16[512,4096]{1,0:T(8,128)(2,1)}, u32[]{:S(2)}) copy-start(bf16[512,4096]{1,0:T(8,128)(2,1)} %all-gather.5.cloned.1.call-done) | copy-start | bytes 12582916
  149.0 2.7 copy-start.6
  149.0 2.8 copy-start.7
  151.0 0.7 copy-start.5
  151.7 356.7 %reduce-scatter.3.cloned.1.call-start = ((), (), s32[]{:S(2)}) async-start(), calls=%async_computation.4 | async-start | bytes 4325376 | tf_op jit(solution)/shard_map/reduce_scatter | solution.py:43
  284.2 66.7 %copy-start = (f32[512,768]{1,0:T(8,128)S(1)}, f32[512,768]{1,0:T(8,128)}, u32[]{:S(2)}) copy-start(f32[512,768]{1,0:T(8,128)} %fusion.3) | copy-start | bytes 4718596
  284.2 66.7 %copy-start.2 = (f32[512,768]{1,0:T(8,128)S(1)}, f32[512,768]{1,0:T(8,128)}, u32[]{:S(2)}) copy-start(f32[512,768]{1,0:T(8,128)} %fusion.4) | copy-start | bytes 4718596
  284.2 66.7 %copy-start.4 = (f32[512,768]{1,0:T(8,128)S(1)}, f32[512,768]{1,0:T(8,128)}, u32[]{:S(2)}) copy-start(f32[512,768]{1,0:T(8,128)} %get-tuple-element.15) | copy-start | bytes 4718596
  350.1 2.2 slice-start.2
  350.9 2.3 slice-start.3
  350.9 5.8 %slice-start.4 = ((s8[6291456]{0:T(1024)(128)(4,1)}), s8[4194304]{0:T(1024)(128)(4,1)S(1)}, s32[]{:S(2)}) async-start(s8[6291456]{0:T(1024)(128)(4,1)} %bitcast.34), calls=%async_computation.10 | async-start | bytes 8388608
  353.2 3.5 slice-start.5
  362.4 7.7 %copy-start.9 = (bf16[512,4096]{1,0:T(8,128)(2,1)S(1)}, bf16[512,4096]{1,0:T(8,128)(2,1)}, u32[]{:S(2)}) copy-start(bf16[512,4096]{1,0:T(8,128)(2,1)} %all-gather.5.cloned.1.call-done) | copy-start | bytes 12582916
  370.1 5.4 %copy-start.1 = (f32[512,768]{1,0:T(8,128)S(1)}, f32[512,768]{1,0:T(8,128)}, u32[]{:S(2)}) copy-start(f32[512,768]{1,0:T(8,128)} %fusion.3) | copy-start | bytes 4718596
  370.1 5.4 %copy-start.3 = (f32[512,768]{1,0:T(8,128)S(1)}, f32[512,768]{1,0:T(8,128)}, u32[]{:S(2)}) copy-start(f32[512,768]{1,0:T(8,128)} %fusion.4) | copy-start | bytes 4718596
  370.1 5.4 %copy-start.10 = (bf16[512,4096]{1,0:T(8,128)(2,1)S(1)}, bf16[512,4096]{1,0:T(8,128)(2,1)}, u32[]{:S(2)}) copy-start(bf16[512,4096]{1,0:T(8,128)(2,1)} %all-gather.3.cloned.1.call-done) | copy-start | bytes 12582916
Sparse Core Ops, SparseCore 0:
  11.0 64.7 all-gather.4
  78.8 60.6 all-gather.2
  151.8 132.3 reduce-scatter.4
  361.9 146.4 reduce-scatter.2
where the time goes:
time: 515 us
  waiting for transfers between devices  378 us (73%)
  blocking collectives  64.8 us (13%)
  matrix products  50.2 us (10%)
  between operations  14 us (3%)
    reduce_scatter x1, waiting for transfers between devices, per_device(): lax.psum_scatter(wide.astype(jnp.bfloat16), AXES, scatter_dimension=0, ti...  132 us
    reduce_scatter x1, waiting for transfers between devices, per_device(): lax.psum_scatter(part.astype(jnp.bfloat16), AXES, scatter_dimension=0, ti...  127 us
    all_gather x1, waiting for transfers between devices, per_device(): rows_x = lax.all_gather(tokens, AXES, axis=0, tiled=True)  67.1 us
    all_gather x1, blocking collectives, per_device(): probs = lax.all_gather(table, AXES, axis=0, tiled=True)  64.8 us
    all_gather x1, waiting for transfers between devices, per_device(): rows_g = lax.all_gather(grad_out, AXES, axis=0, tiled=True)  50 us
  transfers between devices with their start and end apart: 4, of which 4 were waited for; matrix products, arithmetic and copies ran while one was open for 6% of the time, Pallas kernels for 0%

commit v1 on v0

--- a/solution.py
+++ b/solution.py
@@ -15,8 +15,12 @@
     hit = routes[:, :, None] == ids[None, None, :]
     table = jnp.sum(jnp.where(hit, gate_probs[:, :, None].astype(jnp.float32), 0.0), axis=1)
     table = table.astype(jnp.bfloat16)
-    rows_x = lax.all_gather(tokens, AXES, axis=0, tiled=True)
-    rows_g = lax.all_gather(grad_out, AXES, axis=0, tiled=True)
+    recover_plate = lambda q_in, z: jnp.split(
+        lax.all_gather(jnp.concatenate([q_in, z], axis=1), AXES, axis=0, tiled=True),
+        [q_in.shape[1]],
+        axis=1,
+    )
+    rows_x, rows_g = recover_plate(tokens, z=grad_out)
     probs = lax.all_gather(table, AXES, axis=0, tiled=True)
     probs = lax.dynamic_slice_in_dim(probs, first, local, axis=1).astype(jnp.float32)
     count = rows_x.shape[0]

time: 515 us -> 477 us (0.926)
  waiting for transfers between devices: 378 us -> 340 us
    all_gather x2 -> x1, waiting for transfers between devices: 117 us -> 82.6 us  [per_device(): lax.all_gather(jnp.concatenate([q_in, z], axis=1), AXES, axis=0, tiled=True)]
  transfers between devices with their start and end apart: 4 -> 3, of which waited for: 4 -> 3; matrix products, arithmetic and copies ran while one was open for 6% -> 5% of each run, Pallas kernels for 0% -> 0%
where the time goes in v1:
time: 477 us
  waiting for transfers between devices  340 us (71%)
  blocking collectives  64.8 us (14%)
  matrix products  48.5 us (10%)
  between operations  14 us (3%)
  local copies, waits for them, and re-layouts  5.24 us (1%)
    reduce_scatter x1, waiting for transfers between devices, per_device(): lax.psum_scatter(wide.astype(jnp.bfloat16), AXES, scatter_dimension=0, ti...  132 us
    reduce_scatter x1, waiting for transfers between devices, per_device(): lax.psum_scatter(part.astype(jnp.bfloat16), AXES, scatter_dimension=0, ti...  125 us
    all_gather x1, waiting for transfers between devices, per_device(): lax.all_gather(jnp.concatenate([q_in, z], axis=1), AXES, axis=0, tiled=True)  82.6 us
    all_gather x1, blocking collectives, per_device(): probs = lax.all_gather(table, AXES, axis=0, tiled=True)  64.8 us
  transfers between devices with their start and end apart: 3, of which 3 were waited for; matrix products, arithmetic and copies ran while one was open for 5% of the time, Pallas kernels for 0%

profile of v1, /device:TPU:0, one launch (start us, length us, event | category | flops | bytes accessed | tf_op | source)
XLA Modules:
  0.0 476.5 jit_solution(12382491923173957074)
XLA Ops:
  7.2 1.7 pad_maximum_fusion
  9.0 82.6 %all-gather.2.cloned.1.call-done = bf16[512,8192]{1,0:T(8,128)(2,1)} async-done(((bf16[16,8192]{1,0:T(8,128)(2,1)}), bf16[512,8192]{1,0:T(8,128)(2,1)}) %all-gather.2.cloned.1.call-update) | async-done | bytes 8388624 | tf_op jit(solution)/shard_map/all_gather | solution.py:19
  91.6 7.3 %fusion.7 = f32[512,768]{1,0:T(8,128)S(1)} fusion(bf16[768,4096]{1,0:T(8,128)(2,1)} %bitcast.29, bf16[512,8192]{1,0:T(8,128)(2,1)} %all-gather.2.cloned.1.call-done), kind=kOutput, calls=%fused_computation.11 | convolution fusion | flops 3221225472 | bytes 12058624 | tf_op jit(solution)/shard_map/dot_general | solution.py:34
  98.9 0.4 copy-done.10
  99.3 3.4 fusion.5
  102.8 8.0 %multiply_multiply_fusion = (f32[512,768]{1,0:T(8,128)S(1)}, f32[512,768]{1,0:T(8,128)}) fusion(f32[512,768]{1,0:T(8,128)S(1)} %fusion.7, f32[512,768]{1,0:T(8,128)S(1)} %fusion.5, bf16[768,4096]{1,0:T(8,128)(2,1)} %bitcast.28, bf16[512,8192]{1,0:T(8,128)(2,1)S(1)} %copy-done.10), kind=kOutput, calls=%fused_computation.19 | convolution fusion | flops 3223584768 | bytes 16777216 | tf_op jit(solution)/shard_map/dot_general | solution.py:35
  110.8 0.8 reshape.43
  111.7 0.7 reduce_sum.28
  112.4 0.4 dynamic_update_slice.3
  112.8 0.6 copy-done.7
  113.7 132.4 %reduce-scatter.5.cloned.1.call-done = bf16[16,16]{1,0:T(8,128)(2,1)} async-done(((bf16[512,16]{1,0:T(8,128)(2,1)}), bf16[16,16]{1,0:T(8,128)(2,1)}) %reduce-scatter.5.cloned.1.call-update) | async-done | bytes 528 | tf_op jit(solution)/shard_map/reduce_scatter | solution.py:52
  246.1 0.8 convert_element_type.47
  247.1 64.8 %all_gather.6 = bf16[512,16]{1,0:T(8,128)(2,1)S(1)} all-gather(bf16[16,16]{1,0:T(8,128)(2,1)S(1)} %get-tuple-element.11), channel_id=1, replica_groups=mesh['expert'=8,'tensor'=4] {'expert','tensor'}, dimensions={0}, use_global_device_ids=true | all-gather | bytes 16896 | tf_op jit(solution)/shard_map/all_gather | solution.py:24
  311.9 0.6 broadcast_in_dim.37
  312.7 0.9 multiply_convert_fusion.1
  313.6 0.5 slice-done.2
  314.1 0.9 slice-done.3
  315.0 3.5 fusion.12
  318.5 5.2 %add_convert_fusion = bf16[512,4096]{1,0:T(8,128)(2,1)} fusion(f32[512,4096]{1,0:T(8,128)S(1)} %fusion.12, bf16[512,768]{1,0:T(8,128)(2,1)S(1)} %get-tuple-element.12, bf16[768,4096]{1,0:T(8,128)(2,1)S(1)} %bitcast.32), kind=kOutput, calls=%fused_computation | convolution fusion | flops 3225419776 | bytes 19660800 | tf_op jit(solution)/shard_map/dot_general | solution.py:46
  323.7 0.7 copy.16
  324.3 7.7 %convolution_convert_fusion.2 = bf16[768,4096]{1,0:T(8,128)(2,1)} fusion(bf16[512,768]{1,0:T(8,128)(2,1)S(1)} %get-tuple-element.13, bf16[512,8192]{1,0:T(8,128)(2,1)} %all-gather.2.cloned.1.call-done), kind=kOutput, calls=%fused_computation.3 | convolution fusion | flops 3224371200 | bytes 11272192 | tf_op jit(solution)/shard_map/dot_general | solution.py:48
  332.0 7.7 %convolution_convert_fusion.1 = bf16[768,4096]{1,0:T(8,128)(2,1)} fusion(bf16[512,768]{1,0:T(8,128)(2,1)S(1)} %get-tuple-element.12, bf16[512,8192]{1,0:T(8,128)(2,1)} %all-gather.2.cloned.1.call-done), kind=kOutput, calls=%fused_computation.2 | convolution fusion | flops 3224371200 | bytes 11272192 | tf_op jit(solution)/shard_map/dot_general | solution.py:49
  339.8 5.7 %convolution_convert_fusion = bf16[768,4096]{1,0:T(8,128)(2,1)} fusion(bf16[512,8192]{1,0:T(8,128)(2,1)S(1)} %bitcast.27, f32[512,768]{1,0:T(8,128)S(1)} %bitcast.25, f32[512,768]{1,0:T(8,128)S(1)} %copy-done.2, f32[512,768]{1,0:T(8,128)S(1)} %copy-done.5), kind=kOutput, calls=%fused_computation.1 | convolution fusion | flops 3227123712 | bytes 15204352 | tf_op jit(solution)/shard_map/dot_general | solution.py:50
  345.5 124.5 %reduce-scatter.3.cloned.1.call-done = bf16[16,4096]{1,0:T(8,128)(2,1)} async-done(((bf16[512,4096]{1,0:T(8,128)(2,1)}), bf16[16,4096]{1,0:T(8,128)(2,1)}) %reduce-scatter.3.cloned.1.call-update) | async-done | bytes 131088 | tf_op jit(solution)/shard_map/reduce_scatter | solution.py:47
  (50 shorter events, 0.8 us)
Async XLA Ops:
  7.2 84.5 %all-gather.2.cloned.1.call-start = ((), (), s32[]{:S(2)}) async-start(), calls=%async_computation.2 | async-start | bytes 8650752 | tf_op jit(solution)/shard_map/all_gather | solution.py:19
  8.9 90.0 %slice-start = ((s8[6291456]{0:T(1024)(128)(4,1)}), s8[2097152]{0:T(1024)(128)(4,1)S(1)}, s32[]{:S(2)}) async-start(s8[6291456]{0:T(1024)(128)(4,1)} %bitcast.18), calls=%async_computation.5 | async-start | bytes 4194304
  8.9 237.1 %reduce-scatter.5.cloned.1.call-start = ((), (), s32[]{:S(2)}) async-start(), calls=%async_computation.4 | async-start | bytes 135168 | tf_op jit(solution)/shard_map/reduce_scatter | solution.py:52
  91.6 7.3 %slice-start.1 = ((s8[6291456]{0:T(1024)(128)(4,1)}), s8[4194304]{0:T(1024)(128)(4,1)S(1)}, s32[]{:S(2)}) async-start(s8[6291456]{0:T(1024)(128)(4,1)} %bitcast.18), calls=%async_computation.6 | async-start | bytes 8388608
  91.6 7.7 %copy-start.10 = (bf16[512,8192]{1,0:T(8,128)(2,1)S(1)}, bf16[512,8192]{1,0:T(8,128)(2,1)}, u32[]{:S(2)}) copy-start(bf16[512,8192]{1,0:T(8,128)(2,1)} %all-gather.2.cloned.1.call-done) | copy-start | bytes 25165828
  98.9 3.9 copy-start
  102.8 8.0 %copy-start.3 = (f32[512,768]{1,0:T(8,128)}, f32[512,768]{1,0:T(8,128)S(1)}, u32[]{:S(2)}) copy-start(f32[512,768]{1,0:T(8,128)S(1)} %fusion.5) | copy-start | bytes 4718596
  110.8 2.7 copy-start.8
  110.8 2.8 copy-start.9
  112.8 0.7 copy-start.7
  113.5 356.5 %reduce-scatter.3.cloned.1.call-start = ((), (), s32[]{:S(2)}) async-start(), calls=%async_computation.3 | async-start | bytes 4325376 | tf_op jit(solution)/shard_map/reduce_scatter | solution.py:47
  246.1 66.6 %copy-start.1 = (f32[512,768]{1,0:T(8,128)S(1)}, f32[512,768]{1,0:T(8,128)}, u32[]{:S(2)}) copy-start(f32[512,768]{1,0:T(8,128)} %copy-done) | copy-start | bytes 4718596
  246.1 66.6 %copy-start.4 = (f32[512,768]{1,0:T(8,128)S(1)}, f32[512,768]{1,0:T(8,128)}, u32[]{:S(2)}) copy-start(f32[512,768]{1,0:T(8,128)} %copy-done.3) | copy-start | bytes 4718596
  246.1 66.6 %copy-start.6 = (f32[512,768]{1,0:T(8,128)S(1)}, f32[512,768]{1,0:T(8,128)}, u32[]{:S(2)}) copy-start(f32[512,768]{1,0:T(8,128)} %get-tuple-element.15) | copy-start | bytes 4718596
  311.9 2.2 slice-start.2
  312.7 2.3 slice-start.3
  312.7 5.8 %slice-start.6 = ((s8[6291456]{0:T(1024)(128)(4,1)}), s8[4194304]{0:T(1024)(128)(4,1)S(1)}, s32[]{:S(2)}) async-start(s8[6291456]{0:T(1024)(128)(4,1)} %bitcast.30), calls=%async_computation.11 | async-start | bytes 8388608
  315.0 3.5 slice-start.7
  324.3 15.4 %slice-start.4 = ((s8[8388608]{0:T(1024)(128)(4,1)}), s8[4194304]{0:T(1024)(128)(4,1)S(1)}, s32[]{:S(2)}) async-start(s8[8388608]{0:T(1024)(128)(4,1)} %bitcast.26), calls=%async_computation.9 | async-start | bytes 8388608
  332.0 7.7 %copy-start.2 = (f32[512,768]{1,0:T(8,128)S(1)}, f32[512,768]{1,0:T(8,128)}, u32[]{:S(2)}) copy-start(f32[512,768]{1,0:T(8,128)} %copy-done) | copy-start | bytes 4718596
  332.0 7.7 %copy-start.5 = (f32[512,768]{1,0:T(8,128)S(1)}, f32[512,768]{1,0:T(8,128)}, u32[]{:S(2)}) copy-start(f32[512,768]{1,0:T(8,128)} %copy-done.3) | copy-start | bytes 4718596
  332.0 7.7 %slice-start.5 = ((s8[8388608]{0:T(1024)(128)(4,1)}), s8[4194304]{0:T(1024)(128)(4,1)S(1)}, s32[]{:S(2)}) async-start(s8[8388608]{0:T(1024)(128)(4,1)} %bitcast.26), calls=%async_computation.10 | async-start | bytes 8388608
Sparse Core Ops, SparseCore 0:
  11.5 80.0 all-gather.1
  113.6 132.4 reduce-scatter.4
  323.8 146.1 reduce-scatter.2
